TPU v7x, 256 devices: a whole 4x4x8 slice. The times are simulated.
256 devices in a mesh: rcv: 32 (over z, y), hd: 8 (over x, core).
Axes of the slice: x: 4, y: 4, z: 8, core: 2. Of those that a mesh axis runs over, the one named last changes fastest.
Arguments:
- stream: bfloat16 [32768, 1024], P(('rcv', 'hd')), may hold values from -3 to 3
- queries: bfloat16 [32768, 1024], P(('rcv', 'hd')), may hold values from -9 to 9
- keys: bfloat16 [32768, 1024], P(('rcv', 'hd')), may hold values from -9 to 9
- values: bfloat16 [32768, 1024], P(('rcv', 'hd')), may hold values from -6 to 6
- out_proj: bfloat16 [1024, 1024], replicated, may hold values from -0.375 to 0.375
- norm_gain: float32 [1024], replicated, may hold values from 0.5 to 1.5
- expert_weights: bfloat16 [1024, 64, 3, 512], P(None, 'rcv'), may hold values from -0.1875 to 0.1875
- expert_ids: int32 [32768, 4], P(('rcv', 'hd')), may hold values from 0 to 63, as said below
- gate_weights: float32 [32768, 4], P(('rcv', 'hd')), may hold values from 0.1 to 1
- out_cotangent: bfloat16 [32768, 1024], P(('rcv', 'hd')), may hold values from -6 to 6
Outputs:
- block_out: bfloat16 [32768, 1024], P(('rcv', 'hd'))
- stream_grad: bfloat16 [32768, 1024], P(('rcv', 'hd'))
Inputs may be any that keep to these rules, and one draw needn't show every extreme that they name: `expert_ids`: each token names 4 different experts; its k-th id lies in k * 16 to (k + 1) * 16 - 1. Within each aligned block of 128 rows no expert is named more than 10 times, and in each of these 4 ranges one expert, the same for all blocks, is named exactly 10 times in every block.
All inputs are finite; a program needn't handle non-finite values.
Results may differ from a plain program's by a relative error of at most 0.015.
Values may be sent and summed in bfloat16 or wider, within the bound.
A program may use at most 128 MiB of HBM per device.

v0:
```python
import math

import jax
import jax.numpy as jnp
from jax import lax
from jax.sharding import PartitionSpec as P

HS = 64


NORM_EPS = 1e-06


def silu_parts(pre_gate):
    sigmoid = 1.0 / (1.0 + jnp.exp(-pre_gate))
    return (pre_gate * sigmoid, sigmoid * (1.0 + pre_gate * (1.0 - sigmoid)))


def expert_pass(arrived_rows, arrived_cot, expert_weights):
    pre_pair = jnp.einsum(
        "jmd,djcf->jmcf", arrived_rows, expert_weights[:, :, :2], preferred_element_type=jnp.float32
    )
    activated, act_slope = silu_parts(pre_pair[:, :, 0])
    up_value = pre_pair[:, :, 1]
    hidden = (activated * up_value).astype(jnp.bfloat16)
    expert_outs = jnp.einsum(
        "jmf,djf->jmd", hidden, expert_weights[:, :, 2], preferred_element_type=jnp.float32
    ).astype(jnp.bfloat16)
    back_hidden = jnp.einsum(
        "jmd,djf->jmf", arrived_cot, expert_weights[:, :, 2], preferred_element_type=jnp.float32
    )
    hidden_grads = jnp.stack(
        [back_hidden * up_value * act_slope, back_hidden * activated], axis=2
    ).astype(jnp.bfloat16)
    expert_grads = jnp.einsum(
        "jmcf,djcf->jmd", hidden_grads, expert_weights[:, :, :2], preferred_element_type=jnp.float32
    ).astype(jnp.bfloat16)
    return (expert_outs, expert_grads)


def per_device(
    stream,
    queries,
    keys,
    values,
    out_proj,
    norm_gain,
    expert_weights,
    expert_ids,
    gate_weights,
    out_cotangent,
):
    row_count, feature_width = stream.shape
    groups = lax.axis_size("rcv")
    local_count = expert_weights.shape[1]
    experts = local_count * groups
    top_count = expert_ids.shape[1]
    capacity = (5 * row_count * top_count + 4 * experts - 1) // (4 * experts)
    score_scale = 1.0 / math.sqrt(HS)
    flat_ids = expert_ids.reshape(-1)
    onehot = (flat_ids[:, None] == jnp.arange(experts, dtype=jnp.int32)[None, :]).astype(jnp.int32)
    slot_index = jnp.sum((jnp.cumsum(onehot, axis=0) - onehot) * onehot, axis=1)
    owner_rank = flat_ids // local_count
    local_expert = flat_ids % local_count
    cell_index = (local_expert * groups + owner_rank) * capacity + slot_index
    cell_total = experts * capacity
    token_index = jnp.arange(row_count * top_count, dtype=jnp.int32) // top_count
    source = jnp.full((cell_total,), row_count, jnp.int32).at[cell_index].set(token_index)

    def pack_rows(row_data):
        padded = jnp.concatenate([row_data, jnp.zeros((1, feature_width), row_data.dtype)], axis=0)
        return jnp.take(padded, source, axis=0).reshape(
            local_count, groups, capacity, feature_width
        )

    query_all, key_all, value_all = (
        lax.all_to_all(queries, "hd", split_axis=1, concat_axis=0, tiled=True),
        lax.all_to_all(keys, "hd", split_axis=1, concat_axis=0, tiled=True),
        lax.all_to_all(values, "hd", split_axis=1, concat_axis=0, tiled=True),
    )
    length = query_all.shape[0]
    head_count = query_all.shape[1] // HS
    block_rows = math.gcd(length, 512)
    key_heads = key_all.reshape(length, head_count, HS)
    value_heads = value_all.reshape(length, head_count, HS)

    def one_block(row_start):
        query_block = lax.dynamic_slice_in_dim(query_all, row_start, block_rows, 0).reshape(
            block_rows, head_count, HS
        )
        scores = (
            jnp.einsum("qhd,khd->hqk", query_block, key_heads, preferred_element_type=jnp.float32)
            * score_scale
        )
        row_max = jnp.max(scores, axis=2, keepdims=True)
        raw_weights = jnp.exp(scores - row_max)
        row_total = jnp.sum(raw_weights, axis=2)
        mixed_heads = jnp.einsum(
            "hqk,khd->qhd",
            raw_weights.astype(jnp.bfloat16),
            value_heads,
            preferred_element_type=jnp.float32,
        )
        result = mixed_heads / jnp.transpose(row_total)[:, :, None]
        return result.astype(jnp.bfloat16).reshape(block_rows, head_count * HS)

    starts = jnp.arange(length // block_rows, dtype=jnp.int32) * block_rows
    head_result = lax.map(one_block, starts).reshape(length, head_count * HS)
    attended = lax.all_to_all(head_result, "hd", split_axis=0, concat_axis=1, tiled=True)
    projected = jnp.dot(attended, out_proj, preferred_element_type=jnp.float32)
    mix_stream = (stream.astype(jnp.float32) + projected).astype(jnp.bfloat16)
    stream_wide = mix_stream.astype(jnp.float32)
    inverse = lax.rsqrt(jnp.mean(stream_wide * stream_wide, axis=1, keepdims=True) + NORM_EPS)
    normed = (norm_gain * stream_wide * inverse).astype(jnp.bfloat16)
    arrived_rows, arrived_cot = (
        lax.all_to_all(pack_rows(normed), "rcv", split_axis=1, concat_axis=1, tiled=True),
        lax.all_to_all(pack_rows(out_cotangent), "rcv", split_axis=1, concat_axis=1, tiled=True),
    )
    expert_outs, expert_grads = expert_pass(
        arrived_rows.reshape(local_count, groups * capacity, feature_width),
        arrived_cot.reshape(local_count, groups * capacity, feature_width),
        expert_weights,
    )
    back_out, back_grad = (
        lax.all_to_all(
            expert_outs.reshape(local_count, groups, capacity, feature_width),
            "rcv",
            split_axis=1,
            concat_axis=1,
            tiled=True,
        ),
        lax.all_to_all(
            expert_grads.reshape(local_count, groups, capacity, feature_width),
            "rcv",
            split_axis=1,
            concat_axis=1,
            tiled=True,
        ),
    )
    picked_out = jnp.take(back_out.reshape(cell_total, feature_width), cell_index, axis=0).reshape(
        row_count, top_count, feature_width
    )
    picked_grad = jnp.take(
        back_grad.reshape(cell_total, feature_width), cell_index, axis=0
    ).reshape(row_count, top_count, feature_width)
    gate_column = gate_weights[:, :, None]
    block_out = (
        stream_wide + jnp.sum(gate_column * picked_out.astype(jnp.float32), axis=1)
    ).astype(jnp.bfloat16)
    normed_grad = jnp.sum(gate_column * picked_grad.astype(jnp.float32), axis=1)
    weighted = norm_gain * normed_grad
    scaled = stream_wide * inverse
    stream_grad = out_cotangent.astype(jnp.float32) + inverse * (
        weighted - scaled * jnp.mean(weighted * scaled, axis=1, keepdims=True)
    )
    return (block_out, stream_grad.astype(jnp.bfloat16))


def solution(mesh):
    placed = (
        P(("rcv", "hd"), None),
        P(("rcv", "hd"), None),
        P(("rcv", "hd"), None),
        P(("rcv", "hd"), None),
        P(),
        P(),
        P(None, "rcv", None, None),
        P(("rcv", "hd"), None),
        P(("rcv", "hd"), None),
        P(("rcv", "hd"), None),
    )
    return jax.shard_map(
        per_device,
        mesh=mesh,
        in_specs=placed,
        out_specs=(P(("rcv", "hd"), None), P(("rcv", "hd"), None)),
        check_vma=False,
    )
```

profile of v0, /device:TPU:2, one launch (start us, length us, event | category | flops | bytes accessed | tf_op | source)
XLA Modules:
  0.0 262.4 jit_solution(5864382768889885304)
XLA Ops:
  2.6 5.7 %all-to-all-start.1 = ((bf16[128,8,128]{0,2,1:T(8,128)(2,1)}), bf16[128,8,128]{0,2,1:T(8,128)(2,1)S(1)}, u32[]{:S(2)}, u32[]{:S(2)}) async-start(bf16[128,8,128]{0,2,1:T(8,128)(2,1)} %bitcast.8), calls=%async_computation.1 | async-start | bytes 524288 | tf_op jit(solution)/shard_map/all_to_all | solution.py:78
  14.4 4.8 %all-to-all-start.2 = ((bf16[128,8,128]{0,2,1:T(8,128)(2,1)}), bf16[128,8,128]{0,2,1:T(8,128)(2,1)S(1)}, u32[]{:S(2)}, u32[]{:S(2)}) async-start(bf16[128,8,128]{0,2,1:T(8,128)(2,1)} %bitcast.10), calls=%async_computation.2 | async-start | bytes 524288 | tf_op jit(solution)/shard_map/all_to_all | solution.py:79
  20.1 5.1 %all-to-all-done.2 = bf16[128,8,128]{0,2,1:T(8,128)(2,1)S(1)} async-done(((bf16[128,8,128]{0,2,1:T(8,128)(2,1)}), bf16[128,8,128]{0,2,1:T(8,128)(2,1)S(1)}, u32[]{:S(2)}, u32[]{:S(2)}) %all-to-all-start.2) | async-done | bytes 262176 | tf_op jit(solution)/shard_map/all_to_all | solution.py:79
  25.2 4.8 %all-to-all-start = ((bf16[128,8,128]{0,2,1:T(8,128)(2,1)}), bf16[128,8,128]{0,2,1:T(8,128)(2,1)S(1)}, u32[]{:S(2)}, u32[]{:S(2)}) async-start(bf16[128,8,128]{0,2,1:T(8,128)(2,1)} %bitcast.5), calls=%async_computation | async-start | bytes 524288 | tf_op jit(solution)/shard_map/all_to_all | solution.py:77
  36.3 12.5 %while.10 = (s32[]{:T(128)}, bf16[2,512,128]{2,1,0:T(8,128)(2,1)}, s32[2]{0:T(128)S(1)}, bf16[1024,128]{1,0:T(8,128)(2,1)S(1)}, bf16[1024,2,64]{0,2,1:T(8,128)(2...) while((s32[]{:T(128)}, bf16[2,512,128]{2,1,0:T(8,128)(2,1)}, ...), condition=%wide.region_3.4_spmd, body=%wide.region_0.3_spmd.sunk | while | flops 276953088 | bytes 15487659 | solution.py:108
  48.7 4.8 %all-to-all-start.3 = ((bf16[8,128,128]{2,1,0:T(8,128)(2,1)}), bf16[8,128,128]{2,1,0:T(8,128)(2,1)S(1)}, u32[]{:S(2)}, u32[]{:S(2)}) async-start(bf16[8,128,128]{2,1,0:T(8,128)(2,1)} %bitcast.118), calls=%async_computation.3 | async-start | bytes 524288 | tf_op jit(solution)/shard_map/all_to_all | solution.py:109
  53.6 3.5 %gather_fusion.2 = bf16[640,1024]{1,0:T(8,128)(2,1)} fusion(bf16[129,1024]{1,0:T(8,128)(2,1)S(1)} %concatenate.7, s32[1024]{0:T(1024)S(1)} %pad_clamp_fusion.1), kind=kCustom, calls=%fused_computation.2.clone | custom fusion | bytes 2624000 | tf_op jit(solution)/shard_map/jit(_take)/gather | solution.py:72
  61.4 3.5 %gather_fusion = bf16[640,1024]{1,0:T(8,128)(2,1)} fusion(bf16[129,1024]{1,0:T(8,128)(2,1)S(1)} %concatenate.6, s32[1024]{0:T(1024)S(1)} %pad_clamp_fusion.1), kind=kCustom, calls=%fused_computation.clone | custom fusion | bytes 2624000 | tf_op jit(solution)/shard_map/jit(_take)/gather | solution.py:72
  72.3 10.8 %all-to-all-start.4 = ((bf16[2,32,10,1024]{3,0,2,1:T(2,128)(2,1)}), bf16[2,32,10,1024]{3,0,2,1:T(2,128)(2,1)}, u32[]{:S(2)}, u32[]{:S(2)}) async-start(bf16[2,32,10,1024]{3,0,2,1:T(2,128)(2,1)} %copy.78), calls=%async_computation.4 | async-start | bytes 2621440 | tf_op jit(solution)/shard_map/all_to_all | solution.py:116
  86.1 30.3 %all-to-all-done.4 = bf16[2,32,10,1024]{3,0,2,1:T(2,128)(2,1)} async-done(((bf16[2,32,10,1024]{3,0,2,1:T(2,128)(2,1)}), bf16[2,32,10,1024]{3,0,2,1:T(2,128)(2,1)}, u32[]{:S(2)}, u32[]{:S(2)}) %all-to-all-start.4) | async-done | bytes 1310752 | tf_op jit(solution)/shard_map/all_to_all | solution.py:116
  116.4 6.0 %all-to-all-start.6 = ((bf16[2,32,10,1024]{3,0,2,1:T(2,128)(2,1)}), bf16[2,32,10,1024]{3,0,2,1:T(2,128)(2,1)}, u32[]{:S(2)}, u32[]{:S(2)}) async-start(bf16[2,32,10,1024]{3,0,2,1:T(2,128)(2,1)} %copy.85), calls=%async_computation.6 | async-start | bytes 2621440 | tf_op jit(solution)/shard_map/all_to_all | solution.py:117
  122.4 5.1 %slice.22 = bf16[1024,2,2,512]{3,1,2,0:T(2,128)(2,1)S(1)} slice(bf16[1024,2,3,512]{3,1,2,0:T(2,128)(2,1)} %param.22), slice={[0:1024], [0:2], [0:2], [0:512]} | slice | bytes 8388608 | tf_op jit(solution)/shard_map/slice | solution.py:21
  127.4 4.5 %slice.25 = bf16[1024,2,1,512]{3,1,2,0:T(2,128)(2,1)S(1)} slice(bf16[1024,2,3,512]{3,1,2,0:T(2,128)(2,1)} %param.22), slice={[0:1024], [0:2], [2:3], [0:512]} | slice | bytes 4194304 | tf_op jit(solution)/shard_map/slice | solution.py:27
  132.0 5.6 %fusion.16 = f32[2,320,2,512]{3,1,2,0:T(8,128)} fusion(bf16[1024,2,2,512]{3,1,2,0:T(2,128)(2,1)S(1)} %slice.22, bf16[2,320,1024,1]{2,0,1,3:T(2,128)(2,1)} %bitcast.19), kind=kOutput, calls=%fused_computation.18 | convolution fusion | flops 1342177280 | bytes 8126464 | tf_op jit(solution)/shard_map/jmd,djcf->jmcf/dot_general | solution.py:20
  137.6 16.9 %all-to-all-done.6 = bf16[2,32,10,1024]{3,0,2,1:T(2,128)(2,1)} async-done(((bf16[2,32,10,1024]{3,0,2,1:T(2,128)(2,1)}), bf16[2,32,10,1024]{3,0,2,1:T(2,128)(2,1)}, u32[]{:S(2)}, u32[]{:S(2)}) %all-to-all-start.6) | async-done | bytes 1310752 | tf_op jit(solution)/shard_map/all_to_all | solution.py:117
  154.5 3.6 %fusion.32 = (bf16[2,320,1,512]{3,1,0,2:T(8,128)(2,1)S(1)}, bf16[2,320,1,512]{3,1,0,2:T(8,128)(2,1)S(1)}) fusion(f32[2,320,2,512]{3,1,2,0:T(8,128)} %fusion.16, bf16[1024,2,1,512]{3,1,2,0:T(2,128)(2,1)S(1)} %slice.25, bf16[2,320,1024]{2,0,1:T(2,128)(2,1)} %bitcast.24), kind=kOutput, calls=%fused_computation.47 | convolution fusion | flops 675348480 | bytes 7340032 | tf_op jit(solution)/shard_map/jmd,djf->jmf/dot_general | solution.py:29
  162.2 5.9 %all-to-all-start.7 = ((bf16[2,32,10,1024]{3,0,2,1:T(2,128)(2,1)}), bf16[2,32,10,1024]{3,0,2,1:T(2,128)(2,1)S(1)}, u32[]{:S(2)}, u32[]{:S(2)}) async-start(bf16[2,32,10,1024]{3,0,2,1:T(2,128)(2,1)} %bitcast.28), calls=%async_computation.7 | async-start | bytes 2621440 | tf_op jit(solution)/shard_map/all_to_all | solution.py:132
  168.1 3.3 %fusion.22 = bf16[2,320,1024]{2,1,0:T(8,128)(2,1)S(1)} fusion(bf16[1024,2,1,512]{3,1,2,0:T(2,128)(2,1)} %copy-done.7, f32[2,320,2,512]{3,1,2,0:T(8,128)} %fusion.16), kind=kOutput, calls=%fused_computation.26 | convolution fusion | flops 673710080 | bytes 6029312 | tf_op jit(solution)/shard_map/jmf,djf->jmd/dot_general | solution.py:26
  173.8 25.5 %all-to-all-done.7 = bf16[2,32,10,1024]{3,0,2,1:T(2,128)(2,1)S(1)} async-done(((bf16[2,32,10,1024]{3,0,2,1:T(2,128)(2,1)}), bf16[2,32,10,1024]{3,0,2,1:T(2,128)(2,1)S(1)}, u32[]{:S(2)}, u32[]{:S(2)}) %all-to-all-start.7) | async-done | bytes 1310752 | tf_op jit(solution)/shard_map/all_to_all | solution.py:132
  199.3 6.2 %all-to-all-start.5 = ((bf16[2,32,10,1024]{3,0,2,1:T(2,128)(2,1)}), bf16[2,32,10,1024]{3,0,2,1:T(2,128)(2,1)S(1)}, u32[]{:S(2)}, u32[]{:S(2)}) async-start(bf16[2,32,10,1024]{3,0,2,1:T(2,128)(2,1)} %bitcast.23), calls=%async_computation.5 | async-start | bytes 2621440 | tf_op jit(solution)/shard_map/all_to_all | solution.py:125
  210.1 27.3 %all-to-all-done.5 = bf16[2,32,10,1024]{3,0,2,1:T(2,128)(2,1)S(1)} async-done(((bf16[2,32,10,1024]{3,0,2,1:T(2,128)(2,1)}), bf16[2,32,10,1024]{3,0,2,1:T(2,128)(2,1)S(1)}, u32[]{:S(2)}, u32[]{:S(2)}) %all-to-all-start.5) | async-done | bytes 1310752 | tf_op jit(solution)/shard_map/all_to_all | solution.py:125
  247.4 3.2 %select_convert_fusion.1 = (f32[512,1024]{1,0:T(8,128)}, f32[512,1024]{1,0:T(8,128)S(1)}) fusion(bf16[512,1024]{1,0:T(8,128)(2,1)} %gather_fusion.1, pred[512]{0:T(512)(128)(4,1)S(1)} %get-tuple-element.57, bf16[512,1024]{1,0:T(8,128)(2,1)} %gather_fusion.3), kind=kLoop, calls=%fused_computation.45 | loop fusion | flops 2097152 | bytes 6291968 | tf_op jit(solution)/shard_map/convert_element_type | solution.py:148
  250.6 2.8 %reshape.239 = f32[128,4,1024]{2,1,0:T(4,128)} reshape(f32[512,1024]{1,0:T(8,128)} %get-tuple-element.67) | data formatting | bytes 4194304 | tf_op jit(solution)/shard_map/convert_element_type | solution.py:148
  255.1 5.5 %multiply_reduce_fusion.1 = (f32[128,1024]{1,0:T(8,128)S(1)}, f32[128,1024]{1,0:T(8,128)S(1)}) fusion(f32[128,4,1024]{2,1,0:T(4,128)} %reshape.240, f32[128,4]{1,0:T(8,128)S(1)} %copy.73, f32[128,4,1024]{2,1,0:T(4,128)} %reshape.239), kind=kLoop, calls=%fused_computation.22 | loop fusion | flops 1835008 | bytes 5244928 | tf_op jit(solution)/shard_map/reduce_sum | solution.py:150
  (106 shorter events, 62.9 us)
Async XLA Ops:
  0.6 59.1 %copy-start = (bf16[1024,1024]{1,0:T(8,128)(2,1)S(1)}, bf16[1024,1024]{1,0:T(8,128)(2,1)}, u32[]{:S(2)}) copy-start(bf16[1024,1024]{1,0:T(8,128)(2,1)} %param.20) | copy-start | bytes 6291460
  0.6 10.2 %copy-start.10 = (bf16[128,1024]{1,0:T(8,128)(2,1)S(1)}, bf16[128,1024]{1,0:T(8,128)(2,1)}, u32[]{:S(2)}) copy-start(bf16[128,1024]{1,0:T(8,128)(2,1)} %param.19) | copy-start | bytes 786436
  2.6 16.7 %copy-start.11 = (bf16[128,1024]{1,0:T(8,128)(2,1)S(1)}, bf16[128,1024]{1,0:T(8,128)(2,1)}, u32[]{:S(2)}) copy-start(bf16[128,1024]{1,0:T(8,128)(2,1)} %param.17) | copy-start | bytes 786436
  2.6 11.8 %all-to-all-start.1 = ((bf16[128,8,128]{0,2,1:T(8,128)(2,1)}), bf16[128,8,128]{0,2,1:T(8,128)(2,1)S(1)}, u32[]{:S(2)}, u32[]{:S(2)}) async-start(bf16[128,8,128]{0,2,1:T(8,128)(2,1)} %bitcast.8), calls=%async_computation.1 | async-start | bytes 524288 | tf_op jit(solution)/shard_map/all_to_all | solution.py:78
  14.4 10.8 %all-to-all-start.2 = ((bf16[128,8,128]{0,2,1:T(8,128)(2,1)}), bf16[128,8,128]{0,2,1:T(8,128)(2,1)S(1)}, u32[]{:S(2)}, u32[]{:S(2)}) async-start(bf16[128,8,128]{0,2,1:T(8,128)(2,1)} %bitcast.10), calls=%async_computation.2 | async-start | bytes 524288 | tf_op jit(solution)/shard_map/all_to_all | solution.py:79
  25.2 10.9 %all-to-all-start = ((bf16[128,8,128]{0,2,1:T(8,128)(2,1)}), bf16[128,8,128]{0,2,1:T(8,128)(2,1)S(1)}, u32[]{:S(2)}, u32[]{:S(2)}) async-start(bf16[128,8,128]{0,2,1:T(8,128)(2,1)} %bitcast.5), calls=%async_computation | async-start | bytes 524288 | tf_op jit(solution)/shard_map/all_to_all | solution.py:77
  36.3 17.3 %copy-start.8 = (bf16[128,1024]{1,0:T(8,128)(2,1)S(1)}, bf16[128,1024]{1,0:T(8,128)(2,1)}, u32[]{:S(2)}) copy-start(bf16[128,1024]{1,0:T(8,128)(2,1)} %param.25) | copy-start | bytes 786436
  39.8 1.0 copy-start.12
  46.1 1.0 copy-start.12
  48.7 10.9 %all-to-all-start.3 = ((bf16[8,128,128]{2,1,0:T(8,128)(2,1)}), bf16[8,128,128]{2,1,0:T(8,128)(2,1)S(1)}, u32[]{:S(2)}, u32[]{:S(2)}) async-start(bf16[8,128,128]{2,1,0:T(8,128)(2,1)} %bitcast.118), calls=%async_computation.3 | async-start | bytes 524288 | tf_op jit(solution)/shard_map/all_to_all | solution.py:109
  53.6 6.2 %copy-start.13 = (bf16[128,1024]{1,0:T(8,128)(2,1)S(1)}, bf16[128,1024]{1,0:T(8,128)(2,1)}, u32[]{:S(2)}) copy-start(bf16[128,1024]{1,0:T(8,128)(2,1)} %param.16) | copy-start | bytes 786436
  59.8 1.4 copy-start.14
  61.4 3.5 %copy-start.4 = (bf16[640,1024]{1,0:T(8,128)(2,1)S(1)}, bf16[640,1024]{1,0:T(8,128)(2,1)}, u32[]{:S(2)}) copy-start(bf16[640,1024]{1,0:T(8,128)(2,1)} %gather_fusion.2) | copy-start | bytes 3932164
  72.3 44.1 %all-to-all-start.4 = ((bf16[2,32,10,1024]{3,0,2,1:T(2,128)(2,1)}), bf16[2,32,10,1024]{3,0,2,1:T(2,128)(2,1)}, u32[]{:S(2)}, u32[]{:S(2)}) async-start(bf16[2,32,10,1024]{3,0,2,1:T(2,128)(2,1)} %copy.78), calls=%async_computation.4 | async-start | bytes 2621440 | tf_op jit(solution)/shard_map/all_to_all | solution.py:116
  116.4 38.1 %all-to-all-start.6 = ((bf16[2,32,10,1024]{3,0,2,1:T(2,128)(2,1)}), bf16[2,32,10,1024]{3,0,2,1:T(2,128)(2,1)}, u32[]{:S(2)}, u32[]{:S(2)}) async-start(bf16[2,32,10,1024]{3,0,2,1:T(2,128)(2,1)} %copy.85), calls=%async_computation.6 | async-start | bytes 2621440 | tf_op jit(solution)/shard_map/all_to_all | solution.py:117
  127.4 4.6 %copy-start.5 = (bf16[1024,2,2,512]{3,1,2,0:T(2,128)(2,1)}, bf16[1024,2,2,512]{3,1,2,0:T(2,128)(2,1)S(1)}, u32[]{:S(2)}) copy-start(bf16[1024,2,2,512]{3,1,2,0:T(2,128)(2,1)S(1)} %slice.22) | copy-start | bytes 12582916
  132.0 22.5 %copy-start.7 = (bf16[1024,2,1,512]{3,1,2,0:T(2,128)(2,1)}, bf16[1024,2,1,512]{3,1,2,0:T(2,128)(2,1)S(1)}, u32[]{:S(2)}) copy-start(bf16[1024,2,1,512]{3,1,2,0:T(2,128)(2,1)S(1)} %slice.25) | copy-start | bytes 6291460
  154.5 3.6 %copy-start.6 = (bf16[1024,2,2,512]{3,1,2,0:T(2,128)(2,1)S(1)}, bf16[1024,2,2,512]{3,1,2,0:T(2,128)(2,1)}, u32[]{:S(2)}) copy-start(bf16[1024,2,2,512]{3,1,2,0:T(2,128)(2,1)} %copy-done.5) | copy-start | bytes 12582916
  162.2 37.1 %all-to-all-start.7 = ((bf16[2,32,10,1024]{3,0,2,1:T(2,128)(2,1)}), bf16[2,32,10,1024]{3,0,2,1:T(2,128)(2,1)S(1)}, u32[]{:S(2)}, u32[]{:S(2)}) async-start(bf16[2,32,10,1024]{3,0,2,1:T(2,128)(2,1)} %bitcast.28), calls=%async_computation.7 | async-start | bytes 2621440 | tf_op jit(solution)/shard_map/all_to_all | solution.py:132
  199.3 6.2 %copy-start.15 = (f32[128,4]{0,1:T(4,128)S(1)}, f32[128,4]{0,1:T(4,128)}, u32[]{:S(2)}) copy-start(f32[128,4]{0,1:T(4,128)} %param.24) | copy-start | bytes 6148
  199.3 38.1 %all-to-all-start.5 = ((bf16[2,32,10,1024]{3,0,2,1:T(2,128)(2,1)}), bf16[2,32,10,1024]{3,0,2,1:T(2,128)(2,1)S(1)}, u32[]{:S(2)}, u32[]{:S(2)}) async-start(bf16[2,32,10,1024]{3,0,2,1:T(2,128)(2,1)} %bitcast.23), calls=%async_computation.5 | async-start | bytes 2621440 | tf_op jit(solution)/shard_map/all_to_all | solution.py:125
  255.1 5.5 %copy-start.3 = (f32[128,1024]{1,0:T(8,128)S(1)}, f32[128,1024]{1,0:T(8,128)}, u32[]{:S(2)}) copy-start(f32[128,1024]{1,0:T(8,128)} %copy-done.2) | copy-start | bytes 1572868
  255.1 5.7 %copy-start.9 = (bf16[128,1024]{1,0:T(8,128)(2,1)S(1)}, bf16[128,1024]{1,0:T(8,128)(2,1)}, u32[]{:S(2)}) copy-start(bf16[128,1024]{1,0:T(8,128)(2,1)} %param.25) | copy-start | bytes 786436
  260.6 1.8 copy-start.1
  (1 other events, 0.9 us)
where the time goes:
time: 265 us; the launch traced here: 262 us
  waiting for transfers between devices  113 us (43%)
  local copies, waits for them, and re-layouts  61.7 us (23%)
  starting transfers between devices  48.9 us (18%)
  matrix products  18.2 us (7%)
  other arithmetic  16 us (6%)
  loops' own time  3.97 us (1%)
    all_to_all x1, waiting for transfers between devices, per_device(): lax.all_to_all(pack_rows(normed), 'rcv', split_axis=1, concat_axis=1, til...  30.3 us
    all_to_all x1, waiting for transfers between devices, per_device(): lax.all_to_all(expert_outs.reshape(local_count, groups, capacity, feature...  27.3 us
    all_to_all x1, waiting for transfers between devices, per_device(): lax.all_to_all(expert_grads.reshape(local_count, groups, capacity, featur...  25.5 us
    all_to_all x1, waiting for transfers between devices, per_device(): lax.all_to_all(pack_rows(out_cotangent), 'rcv', split_axis=1, concat_axis...  16.9 us
    all_to_all x1, starting transfers between devices, per_device(): lax.all_to_all(pack_rows(normed), 'rcv', split_axis=1, concat_axis=1, til...  10.8 us
    reshape x4, local copies, waits for them, and re-layouts, pack_rows(): jnp.take(padded, source, axis=0)  7.68 us
    gather x2, local copies, waits for them, and re-layouts, pack_rows(): jnp.take(padded, source, axis=0)  6.95 us
    all_to_all x1, starting transfers between devices, per_device(): lax.all_to_all(expert_outs.reshape(local_count, groups, capacity, feature...  6.15 us
  transfers between devices with their start and end apart: 8, of which 8 were waited for; matrix products, arithmetic and copies ran while one was open for 15% of the time, Pallas kernels for 0%

commit v1 on v0

v1 whole, which is shorter than its diff:
```python
import functools
import math

import jax
import jax.numpy as jnp
from jax import lax
from jax.experimental import pallas as pl
from jax.experimental.pallas import tpu as pltpu
from jax.sharding import PartitionSpec as P

HS = 64
NORM_EPS = 1e-06
NY = 4
PADDED = 32
BF = jnp.bfloat16
F32 = jnp.float32
MESH = pl.DeviceIdType.MESH


def ring_chunks(planes):
    order = [0]
    for step in range(1, planes // 2):
        order += [step, planes - step]
    order.append(planes // 2)
    return [order[at : at + 3] for at in range(0, planes, 3)]


def moe_kernel(
    planes,
    cap,
    info_ref,
    rows_ref,
    cot_ref,
    mix_ref,
    inverse_ref,
    gain_ref,
    weights_ref,
    out_ref,
    grad_ref,
    info_all,
    gathered,
    slot_send,
    slot_recv,
    expert_send,
    expert_recv,
    weights,
    back_hidden,
    hidden,
    hidden_grads,
    sum_send,
    sum_recv,
    info_sems,
    gather_send_sems,
    gather_recv_sems,
    slot_sems,
    slot_local_sems,
    expert_sems,
    expert_local_sems,
    sum_send_sems,
    sum_recv_sems,
    weight_sem,
):
    tokens, width = rows_ref.shape
    local_count = weights.shape[0]
    inner = weights.shape[2] // 3
    half = planes // 2
    half_tokens = tokens // 2
    half_width = width // 2
    tile = min(256, half_width)
    chunks = ring_chunks(planes)
    place = {offset: (c, q) for c, chunk in enumerate(chunks) for q, offset in enumerate(chunk)}
    chunk_rows = NY * local_count * PADDED

    me = lax.axis_index("rcv")
    plane = me // NY
    row = lax.rem(me, NY)
    ring = (
        lax.rem(plane + 1, planes) * NY + row,
        lax.rem(plane + planes - 1, planes) * NY + row,
    )
    mates = [lax.rem(row + step, NY) for step in range(1, NY)]

    weight_copy = pltpu.make_async_copy(weights_ref, weights, weight_sem)
    weight_copy.start()

    barrier = pltpu.get_barrier_semaphore()
    for target in ring:
        pl.semaphore_signal(barrier, inc=1, device_id={"rcv": target}, device_id_type=MESH)
    for mate in mates:
        pl.semaphore_signal(
            barrier, inc=1, device_id={"rcv": plane * NY + mate}, device_id_type=MESH
        )
    pl.semaphore_wait(barrier, 2 + len(mates))

    def slot_of(array, offset):
        if offset == 0:
            return (rows_ref, cot_ref)[array]
        return gathered.at[array, offset]

    def ring_offsets(direction, step):
        if direction == 0:
            return step - 1, step
        return (planes - step + 1) % planes, planes - step

    def gather_copy(array, direction, step, piece):
        source, target = ring_offsets(direction, step)
        part = pl.ds(piece * half_tokens, half_tokens)
        return pltpu.make_async_remote_copy(
            src_ref=slot_of(array, source).at[part],
            dst_ref=gathered.at[array, target].at[part],
            send_sem=gather_send_sems.at[array, direction, step - 1, piece],
            recv_sem=gather_recv_sems.at[array, direction, step - 1, piece],
            device_id={"rcv": ring[direction]},
            device_id_type=MESH,
        )

    def info_copy(direction, step):
        source, target = ring_offsets(direction, step)
        return pltpu.make_async_remote_copy(
            src_ref=info_ref if source == 0 else info_all.at[source],
            dst_ref=info_all.at[target],
            send_sem=info_sems.at[0, direction, step - 1],
            recv_sem=info_sems.at[1, direction, step - 1],
            device_id={"rcv": ring[direction]},
            device_id_type=MESH,
        )

    def info_of(offset):
        return info_ref[...] if offset == 0 else info_all[offset]

    def slot_mask(position, cells):
        index = lax.broadcasted_iota(jnp.int32, (chunk_rows, tokens), 0)
        expert = lax.shift_right_logical(index, 5)
        inside = lax.bitwise_and(index, 31) - cap * position
        cell = (plane * (NY * local_count) + expert) * cap + inside
        cell = jnp.where((inside >= 0) & (inside < cap), cell, -1).astype(F32)
        return [cell == cells[k : k + 1, :] for k in range(4)]

    def one_hot(offset):
        info = info_of(offset)
        hits = slot_mask(place[offset][1], info)
        total = jnp.zeros((chunk_rows, tokens), F32)
        for hit in hits:
            total = jnp.where(hit, 1.0, total)
        return total.astype(BF)

    def gate_map(offset):
        info = info_of(offset)
        hits = slot_mask(place[offset][1], info)
        total = jnp.zeros((chunk_rows, tokens), F32)
        for k, hit in enumerate(hits):
            total = jnp.where(hit, info[4 + k : 5 + k, :], total)
        high = total.astype(BF)
        return high, (total - high.astype(F32)).astype(BF)

    def slot_copy(array, c, step):
        mate = mates[step - 1]
        return pltpu.make_async_remote_copy(
            src_ref=slot_send.at[array, c, mate],
            dst_ref=slot_recv.at[array, :, c, row],
            send_sem=slot_sems.at[0, array, c, step - 1],
            recv_sem=slot_sems.at[1, array, c, step - 1],
            device_id={"rcv": plane * NY + mate},
            device_id_type=MESH,
        )

    def slot_local_copy(array, c):
        return pltpu.make_async_copy(
            slot_send.at[array, c, row],
            slot_recv.at[array, :, c, row],
            slot_local_sems.at[array, c],
        )

    def pack(array, c):
        maps = [one_hot(offset) for offset in chunks[c]]
        for at in range(0, width, tile):
            columns = pl.ds(at, tile)
            total = None
            for selector, offset in zip(maps, chunks[c]):
                term = jnp.dot(
                    selector, slot_of(array, offset)[:, columns], preferred_element_type=F32
                )
                total = term if total is None else total + term
            slot_send[array, c, :, :, :, columns] = total.astype(BF).reshape(
                NY, local_count, PADDED, tile
            )
        for step in range(1, NY):
            slot_copy(array, c, step).start()
        slot_local_copy(array, c).start()

    def gather_and_pack(array):
        ready = {0}
        done = 0
        for step in range(1, half + 1):
            for turn in range(2):
                for direction in range(2):
                    piece = direction if turn == 0 else 1 - direction
                    if step == half and turn == 1:
                        continue
                    gather_copy(array, direction, step, piece).wait_recv()
                    if step < half - 1 or (step == half - 1 and piece == direction):
                        gather_copy(array, direction, step + 1, piece).start()
            ready |= {step, planes - step}
            while done < len(chunks) and set(chunks[done]) <= ready:
                pack(array, done)
                done += 1

    for direction in range(2):
        info_copy(direction, 1).start()
    for array in (1, 0):
        for turn in range(2):
            for direction in range(2):
                gather_copy(array, direction, 1, direction if turn == 0 else 1 - direction).start()
    for step in range(1, half + 1):
        for direction in range(2):
            if step == half and direction == 1:
                continue
            info_copy(direction, step).wait_recv()
            if step < half - 1 or (step == half - 1 and direction == 0):
                info_copy(direction, step + 1).start()

    def wait_slots(array):
        for c in range(len(chunks)):
            for step in range(1, NY):
                slot_copy(array, c, step).wait_recv()
            slot_local_copy(array, c).wait()

    gather_and_pack(1)
    gather_and_pack(0)
    weight_copy.wait()
    expert_rows = len(chunks) * NY * PADDED
    inner_tile = min(256, inner)

    wait_slots(1)
    for e in range(local_count):
        cot_rows = slot_recv[1, e].reshape(expert_rows, width)
        for at in range(0, inner, inner_tile):
            back_hidden[e, :, at : at + inner_tile] = jnp.dot(
                cot_rows,
                weights[e, :, 2 * inner + at : 2 * inner + at + inner_tile],
                preferred_element_type=F32,
            )

    def expert_copy(array, c, step):
        mate = mates[step - 1]
        return pltpu.make_async_remote_copy(
            src_ref=expert_send.at[array, :, c, mate],
            dst_ref=expert_recv.at[array, c, row],
            send_sem=expert_sems.at[0, array, c, step - 1],
            recv_sem=expert_sems.at[1, array, c, step - 1],
            device_id={"rcv": plane * NY + mate},
            device_id_type=MESH,
        )

    def expert_local_copy(array, c):
        return pltpu.make_async_copy(
            expert_send.at[array, :, c, row],
            expert_recv.at[array, c, row],
            expert_local_sems.at[array, c],
        )

    def send_experts(array):
        for c in reversed(range(len(chunks))):
            for step in range(1, NY):
                expert_copy(array, c, step).start()
            expert_local_copy(array, c).start()

    contract_last = (((1,), (1,)), ((), ()))
    wait_slots(0)
    for e in range(local_count):
        row_values = slot_recv[0, e].reshape(expert_rows, width)
        for at in range(0, inner, inner_tile):
            gate = jnp.dot(
                row_values, weights[e, :, at : at + inner_tile], preferred_element_type=F32
            )
            up = jnp.dot(
                row_values,
                weights[e, :, inner + at : inner + at + inner_tile],
                preferred_element_type=F32,
            )
            sigmoid = 1.0 / (1.0 + jnp.exp(-gate))
            active = gate * sigmoid
            slope = sigmoid * (1.0 + gate * (1.0 - sigmoid))
            hidden[e, :, at : at + inner_tile] = (active * up).astype(BF)
            back = back_hidden[e, :, at : at + inner_tile]
            hidden_grads[e, :, at : at + inner_tile] = (back * up * slope).astype(BF)
            hidden_grads[e, :, inner + at : inner + at + inner_tile] = (back * active).astype(BF)
        for at in range(0, width, tile):
            result = lax.dot_general(
                hidden[e],
                weights[e, at : at + tile, 2 * inner : 3 * inner],
                contract_last,
                preferred_element_type=F32,
            )
            expert_send[0, e, :, :, :, at : at + tile] = result.astype(BF).reshape(
                len(chunks), NY, PADDED, tile
            )
    send_experts(0)
    for e in range(local_count):
        for at in range(0, width, tile):
            result = lax.dot_general(
                hidden_grads[e],
                weights[e, at : at + tile, 0 : 2 * inner],
                contract_last,
                preferred_element_type=F32,
            )
            expert_send[1, e, :, :, :, at : at + tile] = result.astype(BF).reshape(
                len(chunks), NY, PADDED, tile
            )
    send_experts(1)

    contract_first = (((0,), (0,)), ((), ()))

    def partial(array, offset, maps, at):
        c = place[offset][0]
        block = expert_recv[array, c, :, :, :, at : at + tile].reshape(chunk_rows, tile)
        return lax.dot_general(
            maps[0], block, contract_first, preferred_element_type=F32
        ) + lax.dot_general(maps[1], block, contract_first, preferred_element_type=F32)

    def sum_copy(array, direction, step, piece):
        part = pl.ds(piece * half_width, half_width)
        return pltpu.make_async_remote_copy(
            src_ref=sum_send.at[array, direction, step - 1, :, part],
            dst_ref=sum_recv.at[array, direction, step - 1, :, part],
            send_sem=sum_send_sems.at[array, direction, step - 1, piece],
            recv_sem=sum_recv_sems.at[array, direction, step - 1, piece],
            device_id={"rcv": ring[direction]},
            device_id_type=MESH,
        )

    arrived = set()

    def wait_experts(array, c):
        if (array, c) in arrived:
            return
        arrived.add((array, c))
        for step in range(1, NY):
            expert_copy(array, c, step).wait_recv()
        expert_local_copy(array, c).wait()

    def home_offset(direction, step):
        distance = half - step + 1
        return planes - distance if direction == 0 else distance

    def sum_step(array, direction, step):
        offset = home_offset(direction, step)
        wait_experts(array, place[offset][0])
        maps = gate_map(offset)
        pieces = (direction,) if step == 1 else (direction, 1 - direction)
        for piece in pieces:
            added = step > 2 or (step == 2 and piece == direction)
            if added:
                sum_copy(array, direction, step - 1, piece).wait_recv()
            for at in range(piece * half_width, (piece + 1) * half_width, tile):
                total = partial(array, offset, maps, at)
                if added:
                    total = total + sum_recv[
                        array, direction, step - 2, :, at : at + tile
                    ].astype(F32)
                sum_send[array, direction, step - 1, :, at : at + tile] = total.astype(BF)
            sum_copy(array, direction, step, piece).start()

    for step in range(1, half + 1):
        for array in range(2):
            for direction in range(2):
                sum_step(array, direction, step)

    maps = gate_map(0)

    def final_sum(array):
        wait_experts(array, place[0][0])
        terms = [partial(array, 0, maps, at) for at in range(0, width, tile)]
        total = jnp.concatenate(terms, axis=1)
        for direction in range(2):
            for piece in range(2):
                sum_copy(array, direction, half, piece).wait_recv()
        for direction in range(2):
            total = total + sum_recv[array, direction, half - 1].astype(F32)
        return total

    wide = mix_ref[...].astype(F32)
    out_ref[...] = (wide + final_sum(0)).astype(BF)
    weighted = gain_ref[...] * final_sum(1)
    inverse = inverse_ref[...]
    scaled = wide * inverse
    mean = jnp.mean(weighted * scaled, axis=1, keepdims=True)
    grad_ref[...] = (cot_ref[...].astype(F32) + inverse * (weighted - scaled * mean)).astype(BF)

    for direction in range(2):
        for step in range(1, half + 1):
            if step < half or direction == 0:
                info_copy(direction, step).wait_send()
            for array in range(2):
                for piece in range(2):
                    if step < half or piece == direction:
                        gather_copy(array, direction, step, piece).wait_send()
                    if step > 1 or piece == direction:
                        sum_copy(array, direction, step, piece).wait_send()
    for array in range(2):
        for c in range(len(chunks)):
            for step in range(1, NY):
                slot_copy(array, c, step).wait_send()
                expert_copy(array, c, step).wait_send()


def moe(info, rows, cot, mix, inverse, gain, weights, cap):
    planes = lax.axis_size("rcv") // NY
    tokens, width = rows.shape
    local_count, _, wide_inner = weights.shape
    inner = wide_inner // 3
    half = planes // 2
    chunk_count = len(ring_chunks(planes))
    vmem = pl.BlockSpec(memory_space=pltpu.VMEM)
    dma = pltpu.SemaphoreType.DMA
    expert_rows = chunk_count * NY * PADDED
    return pl.pallas_call(
        functools.partial(moe_kernel, planes, cap),
        out_shape=(
            jax.ShapeDtypeStruct((tokens, width), BF),
            jax.ShapeDtypeStruct((tokens, width), BF),
        ),
        in_specs=[vmem] * 6 + [pl.BlockSpec(memory_space=pl.ANY)],
        out_specs=(vmem, vmem),
        scratch_shapes=[
            pltpu.VMEM((planes, 8, tokens), F32),
            pltpu.VMEM((2, planes, tokens, width), BF),
            pltpu.VMEM((2, chunk_count, NY, local_count, PADDED, width), BF),
            pltpu.VMEM((2, local_count, chunk_count, NY, PADDED, width), BF),
            pltpu.VMEM((2, local_count, chunk_count, NY, PADDED, width), BF),
            pltpu.VMEM((2, chunk_count, NY, local_count, PADDED, width), BF),
            pltpu.VMEM(weights.shape, BF),
            pltpu.VMEM((local_count, expert_rows, inner), F32),
            pltpu.VMEM((local_count, expert_rows, inner), BF),
            pltpu.VMEM((local_count, expert_rows, 2 * inner), BF),
            pltpu.VMEM((2, 2, half, tokens, width), BF),
            pltpu.VMEM((2, 2, half, tokens, width), BF),
            dma((2, 2, half)),
            dma((2, 2, half, 2)),
            dma((2, 2, half, 2)),
            dma((2, 2, chunk_count, NY - 1)),
            dma((2, chunk_count)),
            dma((2, 2, chunk_count, NY - 1)),
            dma((2, chunk_count)),
            dma((2, 2, half, 2)),
            dma((2, 2, half, 2)),
            dma(()),
        ],
        compiler_params=pltpu.CompilerParams(
            collective_id=1, has_side_effects=True, vmem_limit_bytes=60 * 1024 * 1024
        ),
        name="moe",
    )(info, rows, cot, mix, inverse, gain, weights)


def routing_info(expert_ids, gate_weights, cap):
    rows = expert_ids.shape[0]
    ids = expert_ids.T
    earlier = jnp.arange(rows)[None, :] < jnp.arange(rows)[:, None]
    same = (ids[:, :, None] == ids[:, None, :]) & earlier[None]
    slot = jnp.sum(same.astype(F32), axis=2)
    cell = ids.astype(F32) * cap + slot
    return jnp.concatenate([cell, gate_weights.T], axis=0)


def per_device(
    stream,
    queries,
    keys,
    values,
    out_proj,
    norm_gain,
    expert_weights,
    expert_ids,
    gate_weights,
    out_cotangent,
):
    row_count, feature_width = stream.shape
    groups = lax.axis_size("rcv")
    local_count = expert_weights.shape[1]
    experts = local_count * groups
    top_count = expert_ids.shape[1]
    cap = (5 * row_count * top_count + 4 * experts - 1) // (4 * experts)
    score_scale = 1.0 / math.sqrt(HS)
    info = routing_info(expert_ids, gate_weights, cap)
    inner = expert_weights.shape[3]
    weights = jnp.transpose(expert_weights, (1, 0, 2, 3)).reshape(
        local_count, feature_width, 3 * inner
    )

    query_all, key_all, value_all = (
        lax.all_to_all(queries, "hd", split_axis=1, concat_axis=0, tiled=True),
        lax.all_to_all(keys, "hd", split_axis=1, concat_axis=0, tiled=True),
        lax.all_to_all(values, "hd", split_axis=1, concat_axis=0, tiled=True),
    )
    length = query_all.shape[0]
    head_count = query_all.shape[1] // HS
    block_rows = math.gcd(length, 512)
    key_heads = key_all.reshape(length, head_count, HS)
    value_heads = value_all.reshape(length, head_count, HS)

    def one_block(row_start):
        query_block = lax.dynamic_slice_in_dim(query_all, row_start, block_rows, 0).reshape(
            block_rows, head_count, HS
        )
        scores = (
            jnp.einsum("qhd,khd->hqk", query_block, key_heads, preferred_element_type=F32)
            * score_scale
        )
        row_max = jnp.max(scores, axis=2, keepdims=True)
        raw_weights = jnp.exp(scores - row_max)
        row_total = jnp.sum(raw_weights, axis=2)
        mixed_heads = jnp.einsum(
            "hqk,khd->qhd", raw_weights.astype(BF), value_heads, preferred_element_type=F32
        )
        result = mixed_heads / jnp.transpose(row_total)[:, :, None]
        return result.astype(BF).reshape(block_rows, head_count * HS)

    starts = jnp.arange(length // block_rows, dtype=jnp.int32) * block_rows
    head_result = lax.map(one_block, starts).reshape(length, head_count * HS)
    attended = lax.all_to_all(head_result, "hd", split_axis=0, concat_axis=1, tiled=True)
    projected = jnp.dot(attended, out_proj, preferred_element_type=F32)
    mix_stream = (stream.astype(F32) + projected).astype(BF)
    stream_wide = mix_stream.astype(F32)
    inverse = lax.rsqrt(jnp.mean(stream_wide * stream_wide, axis=1, keepdims=True) + NORM_EPS)
    normed = (norm_gain * stream_wide * inverse).astype(BF)
    return moe(
        info, normed, out_cotangent, mix_stream, inverse, norm_gain[None, :], weights, cap
    )


def solution(mesh):
    split = P(("rcv", "hd"), None)
    placed = (split,) * 4 + (P(), P(), P(None, "rcv", None, None)) + (split,) * 3
    return jax.shard_map(
        per_device, mesh=mesh, in_specs=placed, out_specs=(split, split), check_vma=False
    )
```

time: 265 us -> 215 us (0.81)
  Pallas kernels: 0 us -> 128 us
  waiting for transfers between devices: 113 us -> 14.9 us
  starting transfers between devices: 48.9 us -> 19.9 us
  local copies, waits for them, and re-layouts: 61.7 us -> 38.4 us
  matrix products: 18.2 us -> 4.09 us
  other arithmetic: 16 us -> 3.53 us
    pallas_call x0 -> x1, Pallas kernels: none -> 128 us  [moe(): pl.pallas_call(functools.partial(moe_kernel, planes, cap), out_shape=(jax...]
    all_to_all x4 -> x0, waiting for transfers between devices: 100 us -> none  [the longest x1 30.3 us: per_device(): lax.all_to_all(pack_rows(normed), 'rcv', split_axis=1, concat_axis=1, til...]
    all_to_all x4 -> x0, starting transfers between devices: 28.9 us -> none  [the longest x1 10.8 us: per_device(): lax.all_to_all(pack_rows(normed), 'rcv', split_axis=1, concat_axis=1, til...]
    unnamed x35 -> x18, local copies, waits for them, and re-layouts: 5.98 us -> 25 us
    dot_general x7 -> x3, matrix products: 16.5 us -> 2.42 us  [the longest x2 1.86 us: one_block(): jnp.einsum('hqk,khd->qhd', raw_weights.astype(BF), value_heads, preferred...]
    gather x4 -> x0, local copies, waits for them, and re-layouts: 12.5 us -> none  [the longest x2 6.95 us: pack_rows(): jnp.take(padded, source, axis=0)]
    slice x3 -> x0, local copies, waits for them, and re-layouts: 9.85 us -> none  [the longest x1 5.07 us: expert_pass(): expert_weights[:, :, :2]]
    convert_element_type x4 -> x0, local copies, waits for them, and re-layouts: 9.33 us -> none  [the longest x1 2.85 us: per_device(): picked_out.astype(jnp.float32)]
  transfers between devices with their start and end apart: 8 -> 4, of which waited for: 8 -> 3; matrix products, arithmetic and copies ran while one was open for 15% -> 14% of each run, Pallas kernels for 0% -> 0%
where the time goes in v1:
time: 215 us; the launch traced here: 213 us
  Pallas kernels  128 us (60%)
  local copies, waits for them, and re-layouts  38.4 us (18%)
  starting transfers between devices  19.9 us (9%)
  waiting for transfers between devices  14.9 us (7%)
  matrix products  4.09 us (2%)
  loops' own time  3.96 us (2%)
  other arithmetic  3.53 us (2%)
    pallas_call x1, Pallas kernels, moe(): pl.pallas_call(functools.partial(moe_kernel, planes, cap), out_shape=(jax...  128 us
    unnamed x18, local copies, waits for them, and re-layouts  25 us
    reshape x1, local copies, waits for them, and re-layouts, per_device(): jnp.transpose(expert_weights, (1, 0, 2, 3))  8.64 us
    all_to_all x1, starting transfers between devices, per_device(): lax.all_to_all(keys, 'hd', split_axis=1, concat_axis=0, tiled=True)  5.56 us
    all_to_all x1, waiting for transfers between devices, per_device(): lax.all_to_all(head_result, 'hd', split_axis=0, concat_axis=1, tiled=True)  5.47 us
    all_to_all x1, waiting for transfers between devices, per_device(): lax.all_to_all(queries, 'hd', split_axis=1, concat_axis=0, tiled=True)  5.19 us
    all_to_all x1, starting transfers between devices, per_device(): lax.all_to_all(queries, 'hd', split_axis=1, concat_axis=0, tiled=True)  4.83 us
    all_to_all x1, starting transfers between devices, per_device(): lax.all_to_all(head_result, 'hd', split_axis=0, concat_axis=1, tiled=True)  4.79 us
  transfers between devices with their start and end apart: 4, of which 3 were waited for; matrix products, arithmetic and copies ran while one was open for 14% of the time, Pallas kernels for 0%

profile of v1, /device:TPU:2, one launch (start us, length us, event | category | flops | bytes accessed | tf_op | source)
XLA Modules:
  0.0 213.2 jit_solution(870292908211522898)
XLA Ops:
  0.6 1.9 copy.47
  2.6 5.6 %all-to-all-start.1 = ((bf16[128,8,128]{0,2,1:T(8,128)(2,1)}), bf16[128,8,128]{0,2,1:T(8,128)(2,1)S(1)}, u32[]{:S(2)}, u32[]{:S(2)}) async-start(bf16[128,8,128]{0,2,1:T(8,128)(2,1)} %bitcast.10), calls=%async_computation.1 | async-start | bytes 524288 | tf_op jit(solution)/shard_map/all_to_all | solution.py:493
  8.1 1.8 copy.49
  9.9 4.3 %all-to-all-done.1 = bf16[128,8,128]{0,2,1:T(8,128)(2,1)S(1)} async-done(((bf16[128,8,128]{0,2,1:T(8,128)(2,1)}), bf16[128,8,128]{0,2,1:T(8,128)(2,1)S(1)}, u32[]{:S(2)}, u32[]{:S(2)}) %all-to-all-start.1) | async-done | bytes 262176 | tf_op jit(solution)/shard_map/all_to_all | solution.py:493
  14.2 4.8 %all-to-all-start.2 = ((bf16[128,8,128]{0,2,1:T(8,128)(2,1)}), bf16[128,8,128]{0,2,1:T(8,128)(2,1)S(1)}, u32[]{:S(2)}, u32[]{:S(2)}) async-start(bf16[128,8,128]{0,2,1:T(8,128)(2,1)} %bitcast.12), calls=%async_computation.2 | async-start | bytes 524288 | tf_op jit(solution)/shard_map/all_to_all | solution.py:494
  19.0 1.8 copy.45
  20.8 16.1 %copy.54 = bf16[1024,2,3,512]{0,3,2,1:T(8,128)(2,1)} copy(bf16[1024,2,3,512]{3,1,2,0:T(2,128)(2,1)} %param.18) | data formatting | bytes 12582912 | tf_op args[6]
  36.9 8.6 %copy.56.weights_ref = bf16[2,1024,1536]{2,1,0:T(8,128)(2,1)} copy(bf16[2,1024,1536]{1,2,0:T(8,128)(2,1)} %bitcast.55) | data formatting | bytes 12582912 | tf_op jit(solution)/shard_map/reshape | solution.py:487
  45.6 4.8 %all-to-all-start = ((bf16[128,8,128]{0,2,1:T(8,128)(2,1)}), bf16[128,8,128]{0,2,1:T(8,128)(2,1)S(1)}, u32[]{:S(2)}, u32[]{:S(2)}) async-start(bf16[128,8,128]{0,2,1:T(8,128)(2,1)} %bitcast.7), calls=%async_computation | async-start | bytes 524288 | tf_op jit(solution)/shard_map/all_to_all | solution.py:492
  51.3 5.2 %all-to-all-done = bf16[128,8,128]{0,2,1:T(8,128)(2,1)S(1)} async-done(((bf16[128,8,128]{0,2,1:T(8,128)(2,1)}), bf16[128,8,128]{0,2,1:T(8,128)(2,1)S(1)}, u32[]{:S(2)}, u32[]{:S(2)}) %all-to-all-start) | async-done | bytes 262176 | tf_op jit(solution)/shard_map/all_to_all | solution.py:492
  56.7 12.4 %while.10 = (s32[]{:T(128)}, bf16[2,512,128]{2,1,0:T(8,128)(2,1)}, s32[2]{0:T(128)S(1)}, bf16[1024,128]{1,0:T(8,128)(2,1)S(1)}, bf16[1024,2,64]{0,2,1:T(8,128)(2...) while((s32[]{:T(128)}, bf16[2,512,128]{2,1,0:T(8,128)(2,1)}, ...), condition=%wide.region_4.5_spmd, body=%wide.region_1.4_spmd.sunk | while | flops 276953088 | bytes 14439055 | solution.py:520
  59.4 0.8 multiply_reduce_fusion.2
  60.2 0.9 fusion.34
  61.2 0.9 fusion.35
  65.6 0.8 multiply_reduce_fusion.2
  66.4 0.9 fusion.34
  67.4 0.9 fusion.35
  69.1 4.8 %all-to-all-start.3 = ((bf16[8,128,128]{2,1,0:T(8,128)(2,1)}), bf16[8,128,128]{2,1,0:T(8,128)(2,1)S(1)}, u32[]{:S(2)}, u32[]{:S(2)}) async-start(bf16[8,128,128]{2,1,0:T(8,128)(2,1)} %bitcast.63), calls=%async_computation.3 | async-start | bytes 524288 | tf_op jit(solution)/shard_map/all_to_all | solution.py:521
  74.5 5.5 %all-to-all-done.3 = bf16[8,128,128]{2,1,0:T(8,128)(2,1)S(1)} async-done(((bf16[8,128,128]{2,1,0:T(8,128)(2,1)}), bf16[8,128,128]{2,1,0:T(8,128)(2,1)S(1)}, u32[]{:S(2)}, u32[]{:S(2)}) %all-to-all-start.3) | async-done | bytes 262176 | tf_op jit(solution)/shard_map/all_to_all | solution.py:521
  80.8 0.7 copy.55.inverse_ref
  81.5 0.8 fusion.16.rows_ref
  82.3 127.6 %moe.1 = (bf16[128,1024]{1,0:T(8,128)(2,1)}, bf16[128,1024]{1,0:T(8,128)(2,1)}) custom-call(f32[8,128]{1,0:T(8,128)} %pad_maximum_fusion.info_ref, bf16[128,1024]{1,0:T(8,128)(2,1)} %fusion.16.rows_ref, bf16[128,1024]{1,0:T(8,128)(2,1)} %cot_ref.1, bf16[128,1024]{1,0:T(8,128)(2,1)} %copy-done.1, f32[128,1]{1,0:T(8,128)} %copy.55.inverse_ref, ...), custom_call_target="tpu_custom_call" | custom-call | tf_op jit(solution)/shard_map/moe/pallas_call | solution.py:417
  209.9 1.7 copy.73
  211.5 1.7 copy.74
  (37 shorter events, 5.5 us)
Async XLA Ops:
  0.6 79.5 %copy-start = (bf16[1024,1024]{1,0:T(8,128)(2,1)S(1)}, bf16[1024,1024]{1,0:T(8,128)(2,1)}, u32[]{:S(2)}) copy-start(bf16[1024,1024]{1,0:T(8,128)(2,1)} %param.16) | copy-start | bytes 6291460
  2.6 11.6 %all-to-all-start.1 = ((bf16[128,8,128]{0,2,1:T(8,128)(2,1)}), bf16[128,8,128]{0,2,1:T(8,128)(2,1)S(1)}, u32[]{:S(2)}, u32[]{:S(2)}) async-start(bf16[128,8,128]{0,2,1:T(8,128)(2,1)} %bitcast.10), calls=%async_computation.1 | async-start | bytes 524288 | tf_op jit(solution)/shard_map/all_to_all | solution.py:493
  14.2 31.4 %all-to-all-start.2 = ((bf16[128,8,128]{0,2,1:T(8,128)(2,1)}), bf16[128,8,128]{0,2,1:T(8,128)(2,1)S(1)}, u32[]{:S(2)}, u32[]{:S(2)}) async-start(bf16[128,8,128]{0,2,1:T(8,128)(2,1)} %bitcast.12), calls=%async_computation.2 | async-start | bytes 524288 | tf_op jit(solution)/shard_map/all_to_all | solution.py:494
  36.9 13.5 %copy-start.3 = (s32[128,4]{0,1:T(4,128)S(1)}, s32[128,4]{0,1:T(4,128)}, u32[]{:S(2)}) copy-start(s32[128,4]{0,1:T(4,128)} %param.19) | copy-start | bytes 6148
  45.6 10.9 %all-to-all-start = ((bf16[128,8,128]{0,2,1:T(8,128)(2,1)}), bf16[128,8,128]{0,2,1:T(8,128)(2,1)S(1)}, u32[]{:S(2)}, u32[]{:S(2)}) async-start(bf16[128,8,128]{0,2,1:T(8,128)(2,1)} %bitcast.7), calls=%async_computation | async-start | bytes 524288 | tf_op jit(solution)/shard_map/all_to_all | solution.py:492
  56.7 17.2 %copy-start.5 = (f32[128,4]{0,1:T(4,128)S(1)}, f32[128,4]{0,1:T(4,128)}, u32[]{:S(2)}) copy-start(f32[128,4]{0,1:T(4,128)} %param.20) | copy-start | bytes 6148
  56.7 23.5 %copy-start.2 = (bf16[128,1024]{1,0:T(8,128)(2,1)S(1)}, bf16[128,1024]{1,0:T(8,128)(2,1)}, u32[]{:S(2)}) copy-start(bf16[128,1024]{1,0:T(8,128)(2,1)} %param.12) | copy-start | bytes 786436
  56.7 24.8 %copy-start.4 = (f32[1024]{0:T(1024)S(1)}, f32[1024]{0:T(1024)}, u32[]{:S(2)}) copy-start(f32[1024]{0:T(1024)} %param.17) | copy-start | bytes 12292
  69.1 10.9 %all-to-all-start.3 = ((bf16[8,128,128]{2,1,0:T(8,128)(2,1)}), bf16[8,128,128]{2,1,0:T(8,128)(2,1)S(1)}, u32[]{:S(2)}, u32[]{:S(2)}) async-start(bf16[8,128,128]{2,1,0:T(8,128)(2,1)} %bitcast.63), calls=%async_computation.3 | async-start | bytes 524288 | tf_op jit(solution)/shard_map/all_to_all | solution.py:521
  80.7 1.6 copy-start.1
